TPU v7x, 32 devices: a whole 2x2x4 slice. The times are simulated.
32 devices in a mesh: seq: 8 (over z, x), tp: 4 (over y, core).
Axes of the slice: x: 2, y: 2, z: 4, core: 2. Of those that a mesh axis runs over, the one named last changes fastest.
Arguments:
- hidden_new: bfloat16 [3, 16, 8192], P(None, None, 'seq'), may hold values from -6 to 6
- w_kv: bfloat16 [8192, 8, 256], P('seq', 'tp'), may hold values from -0.0625 to 0.0625
- w_out: bfloat16 [8192, 8192], P('tp', 'seq'), may hold values from -0.0625 to 0.0625
- queries_draft: bfloat16 [3, 4, 8, 32, 128], P(None, None, 'tp'), may hold values from -48 to 48
- queries_verify: bfloat16 [3, 4, 8, 32, 128], P(None, None, 'tp'), may hold values from -48 to 48
- keys_cache: bfloat16 [4, 8, 16384, 128], P(None, 'tp', 'seq'), may hold values from -6 to 6
- values_cache: bfloat16 [4, 8, 16384, 128], P(None, 'tp', 'seq'), may hold values from -6 to 6
- key_levels: bfloat16 [4, 8, 16384, 128], P(None, 'tp', 'seq'), may hold values from -8 to 7, as said below
- value_levels: bfloat16 [4, 8, 16384, 128], P(None, 'tp', 'seq'), may hold values from -8 to 7, as said below
- key_scales: float32 [4, 8, 16384], P(None, 'tp', 'seq'), may hold values from 0.05 to 0.5
- value_scales: float32 [4, 8, 16384], P(None, 'tp', 'seq'), may hold values from 0.1 to 0.4
- lengths: int32 [4], replicated, may hold values from 2 to 16376, as said below
- accepted: int32 [2, 4], replicated, may hold values from 0 to 4, as said below
Outputs:
- layer_out: bfloat16 [3, 2, 16, 8192], P(None, None, None, 'seq')
Inputs may be any that keep to these rules, and one draw needn't show every extreme that they name: `key_levels`: every entry is a whole number. Positions 0 and 1 of every sequence and head hold equal levels. `value_levels`: every entry is a whole number. `lengths`: some sequence starts with exactly 16376 valid positions, another with 16 or fewer. `accepted`: the values 0 and 4 both occur.
All inputs are finite; a program needn't handle non-finite values.
Results may differ from a plain program's by a relative error of at most 0.006.
The roundings to bfloat16 on the way count: a program that leaves them out, or rounds other values in their place, can miss the bound.
Values may be sent and summed in bfloat16 or wider, within the bound.
A program may use at most 128 MiB of HBM per device.

v0:
```python
import math
import jax
import jax.numpy as jnp
from jax import lax
from jax.sharding import PartitionSpec as P

HD = 128
GROUP = 8
R = 4
ROUNDS = 3
NEG = -1e30


def dequantize(levels, scales):
    return (levels.astype(jnp.float32) * scales[..., None]).astype(jnp.bfloat16)


def attend(queries, keys, values, usable):
    scores = jnp.einsum("bhqd,bhkd->bhqk", queries, keys, preferred_element_type=jnp.float32) * (
        1.0 / math.sqrt(HD)
    )
    scores = jnp.where(usable, scores, NEG)
    maxima = jnp.max(scores, axis=-1)
    weights = jnp.where(usable, jnp.exp(scores - maxima[..., None]), 0.0).astype(jnp.bfloat16)
    totals = jnp.sum(weights.astype(jnp.float32), axis=-1)
    weighted = jnp.einsum("bhqk,bhkd->bhqd", weights, values, preferred_element_type=jnp.float32)
    return (maxima, totals, weighted)


def combine(former, latter):
    highest = jnp.maximum(former[0], latter[0])
    former_w = jnp.exp(former[0] - highest)
    latter_w = jnp.exp(latter[0] - highest)
    return (
        highest,
        former[1] * former_w + latter[1] * latter_w,
        former[2] * former_w[..., None] + latter[2] * latter_w[..., None],
    )


def finish(partial_value):
    return (partial_value[2] / partial_value[1][..., None]).astype(jnp.bfloat16)


def arrange(attended):
    kind_count, batch_size, head_count, query_rows, head_width = attended.shape
    split_rows = attended.reshape(kind_count, batch_size, head_count, GROUP, R, head_width)
    return split_rows.transpose(0, 1, 4, 2, 3, 5).reshape(
        kind_count * batch_size * R, head_count * GROUP * head_width
    )


def stacked_rows(draft_part, verify_part):
    maxima = jnp.stack([draft_part[0], verify_part[0]]).reshape(1, -1)
    totals = jnp.stack([draft_part[1], verify_part[1]]).reshape(1, -1)
    weighted = jnp.stack([draft_part[2], verify_part[2]]).reshape(1, maxima.shape[1], -1)
    return (maxima, totals, weighted)


def spread_merge(draft_part, verify_part, draft_self, verify_self, seq_index):
    maxima, totals, weighted = stacked_rows(draft_part, verify_part)
    maxima, totals, weighted = (
        lax.all_to_all(maxima, "seq", split_axis=1, concat_axis=0, tiled=True),
        lax.all_to_all(totals, "seq", split_axis=1, concat_axis=0, tiled=True),
        lax.all_to_all(weighted, "seq", split_axis=1, concat_axis=0, tiled=True),
    )
    highest = jnp.max(maxima, axis=0)
    factors = jnp.exp(maxima - highest[None])
    share_part = (
        highest,
        jnp.sum(totals * factors, axis=0),
        jnp.sum(weighted * factors[..., None], axis=0),
    )
    share_rows = highest.shape[0]
    self_max, self_tot, self_sum = stacked_rows(draft_self, verify_self)
    row_start = seq_index * share_rows
    self_share = (
        lax.dynamic_slice_in_dim(self_max[0], row_start, share_rows, 0),
        lax.dynamic_slice_in_dim(self_tot[0], row_start, share_rows, 0),
        lax.dynamic_slice_in_dim(self_sum[0], row_start, share_rows, 0),
    )
    merged = finish(combine(share_part, self_share))
    gathered = lax.all_gather(merged, "seq", axis=0, tiled=True)
    return gathered.reshape((2,) + draft_part[2].shape)


def per_device(
    hidden_new,
    w_kv,
    w_out,
    queries_draft,
    queries_verify,
    keys_cache,
    values_cache,
    key_levels,
    value_levels,
    key_scales,
    value_scales,
    lengths,
    accepted,
):
    batch_size, head_count, local_len, head_width = keys_cache.shape
    seq_index = lax.axis_index("seq")
    first_row = seq_index * local_len
    key_low = dequantize(key_levels, key_scales)
    value_low = dequantize(value_levels, value_scales)
    places = first_row + jnp.arange(local_len, dtype=jnp.int32)
    stored = (places[None, :] < lengths[:, None])[:, None, :, None]
    flat_kv = w_kv.reshape(w_kv.shape[0], -1)
    tokens = jnp.arange(GROUP * R, dtype=jnp.int32) % R
    causal = (tokens[:, None] >= jnp.arange(R, dtype=jnp.int32)[None, :])[None, None]
    offsets = jnp.arange(R, dtype=jnp.int32)[None, :]
    batch_rows = jnp.broadcast_to(jnp.arange(batch_size, dtype=jnp.int32)[:, None], (batch_size, R))
    length_now = lengths
    results = []
    for turn_index in range(ROUNDS):
        partial_kv = jnp.dot(hidden_new[turn_index], flat_kv, preferred_element_type=jnp.float32)
        fresh_rows = (
            lax.psum(partial_kv, "seq")
            .astype(jnp.bfloat16)
            .reshape(batch_size, R, head_count, 2, head_width)
        )
        new_keys = fresh_rows[:, :, :, 0].transpose(0, 2, 1, 3)
        new_values = fresh_rows[:, :, :, 1].transpose(0, 2, 1, 3)
        usable = (places[None, :] < length_now[:, None])[:, None, None, :]
        draft_q = queries_draft[turn_index]
        verify_q = queries_verify[turn_index]
        draft_keys = jnp.where(stored, key_low, keys_cache)
        draft_values = jnp.where(stored, value_low, values_cache)
        draft_part = attend(draft_q, draft_keys, draft_values, usable)
        draft_self = attend(draft_q, new_keys, new_values, causal)
        verify_part = attend(verify_q, keys_cache, values_cache, usable)
        verify_self = attend(verify_q, new_keys, new_values, causal)
        attended = spread_merge(draft_part, verify_part, draft_self, verify_self, seq_index)
        projected = jnp.dot(arrange(attended), w_out, preferred_element_type=jnp.float32)
        summed = lax.psum(projected, "tp")
        results.append(summed.astype(jnp.bfloat16).reshape(2, batch_size * R, -1))
        if turn_index + 1 < ROUNDS:
            accepted_now = accepted[turn_index]
            targets = length_now[:, None] + offsets - first_row
            landing = (offsets < accepted_now[:, None]) & (targets >= 0) & (targets < local_len)
            targets = jnp.where(landing, targets, local_len)
            keys_cache = keys_cache.at[batch_rows, :, targets, :].set(
                fresh_rows[:, :, :, 0], mode="drop"
            )
            values_cache = values_cache.at[batch_rows, :, targets, :].set(
                fresh_rows[:, :, :, 1], mode="drop"
            )
            length_now = length_now + accepted_now
    return jnp.stack(results)


def solution(mesh):
    return jax.shard_map(
        per_device,
        mesh=mesh,
        in_specs=(
            P(None, None, "seq"),
            P("seq", "tp", None),
            P("tp", "seq"),
            P(None, None, "tp", None, None),
            P(None, None, "tp", None, None),
            P(None, "tp", "seq", None),
            P(None, "tp", "seq", None),
            P(None, "tp", "seq", None),
            P(None, "tp", "seq", None),
            P(None, "tp", "seq"),
            P(None, "tp", "seq"),
            P(),
            P(),
        ),
        out_specs=P(None, None, None, "seq"),
        check_vma=False,
    )
```

profile of v0, /device:TPU:0, one launch (start us, length us, event | category | flops | bytes accessed | tf_op | source)
XLA Modules:
  0.0 335.9 jit_solution(9079900889281217494)
XLA Ops:
  0.0 4.6 %copy.174 = bf16[4,2,2048,128]{3,2,1,0:T(8,128)(2,1)} copy(bf16[4,2,2048,128]{3,2,1,0:T(8,128)(2,1)} %param.18) | data formatting | bytes 8388608
  4.6 2.0 copy.175
  6.7 3.9 %fusion.169 = (f32[4,2,32]{2,1,0:T(2,128)S(1)}, f32[4,2,32,2048]{3,2,1,0:T(8,128)S(1)}) fusion(bf16[4,2,2048,128]{3,2,1,0:T(8,128)(2,1)} %copy.174, bf16[3,4,2,32,128]{4,3,2,1,0:T(8,128)(2,1)S(1)} %copy-done.16, pred[4,2048]{1,0:T(4,128)(4,1)S(1)} %get-tuple-element.48), kind=kOutput, calls=%fused_computation.242 | convolution fusion | flops 135790336 | bytes 6366208 | tf_op jit(solution)/shard_map/bhqd,bhkd->bhqk/dot_general | solution.py:19
  10.7 5.9 %fusion.170 = (f32[4,2,32]{2,1,0:T(2,128)S(1)}, f32[4,2,32,2048]{3,2,1,0:T(8,128)S(1)}) fusion(bf16[3,4,2,32,128]{4,3,2,1,0:T(8,128)(2,1)} %param.16, bf16[4,2,2048,128]{3,2,1,0:T(8,128)(2,1)S(1)} %copy-done.2, pred[4,2048]{1,0:T(4,128)(4,1)S(1)} %get-tuple-element.48, f32[4,2,2048]{2,1,0:T(2,128)S(1)} %copy-done.22, bf16[4,2,2048,128]{3,2,1,0:T(8,128)(2,1)} %param.20), kind=kOutput, calls=%fused_computation.243 | convolution fusion | flops 144178944 | bytes 10634240 | tf_op jit(solution)/shard_map/bhqd,bhkd->bhqk/dot_general | solution.py:19
  16.6 0.9 convert_reduce_fusion.5
  18.6 7.3 %all-to-all-start.2 = ((f32[1,8,64]{2,0,1:T(1,128)}), f32[1,8,64]{2,0,1:T(1,128)S(1)}, u32[]{:S(2)}, u32[]{:S(2)}) async-start(f32[1,8,64]{2,0,1:T(1,128)} %all_to_all.104), calls=%async_computation.2 | async-start | bytes 8192 | tf_op jit(solution)/shard_map/all_to_all | solution.py:64
  26.9 38.5 %all-reduce = (bf16[16,512]{1,0:T(8,128)(2,1)S(1)}, bf16[16,512]{1,0:T(8,128)(2,1)S(1)}, bf16[16,512]{1,0:T(8,128)(2,1)S(1)}) all-reduce(f32[16,512]{1,0:T(8,128)S(1)} %fusion.111, f32[16,512]{1,0:T(8,128)S(1)} %fusion.115, f32[16,512]{1,0:T(8,128)S(1)} %fusion.113), channel_id=1, replica_groups=mesh['seq'=8,'tp'=4] {'seq'}, use_global_device_ids=true, to_apply=%region_34.35 | all-reduce | flops 24576 | bytes 147456 | tf_op jit(solution)/shard_map/psum | solution.py:119
  66.8 2.5 scatter_fusion
  69.3 10.5 %copy.76 = bf16[4,2,2048,128]{3,1,2,0:T(2,128)(2,1)} copy(bf16[4,2,2048,128]{3,2,1,0:T(8,128)(2,1)} %scatter_fusion) | data formatting | bytes 8388608 | tf_op jit(solution)/shard_map/scatter | solution.py:143
  80.0 2.6 scatter_fusion.2
  82.6 8.5 %fusion.162 = (f32[4,2,32]{2,1,0:T(2,128)S(1)}, f32[4,2,32,2048]{3,2,1,0:T(8,128)}) fusion(bf16[3,4,2,32,128]{4,3,2,1,0:T(8,128)(2,1)S(1)} %copy-done.21, pred[4,2048]{1,0:T(4,128)(4,1)S(1)} %get-tuple-element.48, bf16[4,2,2048,128]{3,1,2,0:T(2,128)(2,1)} %scatter_fusion.2, f32[4,2,2048]{2,1,0:T(2,128)S(1)} %copy-done.23, ...), kind=kOutput, calls=%fused_computation.235 | convolution fusion | flops 144178944 | bytes 10634240 | tf_op jit(solution)/shard_map/bhqd,bhkd->bhqk/dot_general | solution.py:19
  91.1 2.9 fusion.161
  94.0 6.2 %fusion.168 = (f32[4,2,32]{2,1,0:T(2,128)S(1)}, f32[4,2,32,2048]{3,2,1,0:T(8,128)}) fusion(bf16[3,4,2,32,128]{4,3,2,1,0:T(8,128)(2,1)S(1)} %copy-done.21, bf16[4,2,2048,128]{3,2,1,0:T(8,128)(2,1)S(1)} %copy-done.3, pred[4,2048]{1,0:T(4,128)(4,1)S(1)} %get-tuple-element.48, f32[4,2,2048]{2,1,0:T(2,128)S(1)} %copy-done.23, ...), kind=kOutput, calls=%fused_computation.241 | convolution fusion | flops 144178944 | bytes 10634240 | tf_op jit(solution)/shard_map/bhqd,bhkd->bhqk/dot_general | solution.py:19
  100.2 2.8 fusion.167
  103.1 0.9 convolution_bitcast_fusion.1
  104.7 1.2 copy-done.20
  105.9 4.2 %fusion.66 = f32[1,4,2,32,128]{4,3,2,1,0:T(8,128)S(1)} fusion(bf16[4,2,2048,128]{3,2,1,0:T(8,128)(2,1)S(1)} %copy-done, pred[4,2048]{1,0:T(4,128)(4,1)S(1)} %get-tuple-element.48, f32[4,2,2048]{2,1,0:T(2,128)S(1)} %copy-done.24, bf16[4,2,2048,128]{3,2,1,0:T(8,128)(2,1)S(1)} %copy-done.20, f32[4,2,32,2048]{3,2,1,0:T(8,128)S(1)} %copy-done.9, ...), kind=kOutput, calls=%fused_computation.62 | convolution fusion | flops 144179200 | bytes 10691584 | tf_op jit(solution)/shard_map/bhqk,bhkd->bhqd/dot_general | solution.py:26
  110.9 2.5 scatter_fusion.1
  113.4 10.6 %copy.80 = bf16[4,2,2048,128]{3,1,2,0:T(2,128)(2,1)} copy(bf16[4,2,2048,128]{3,2,1,0:T(8,128)(2,1)} %scatter_fusion.1) | data formatting | bytes 8388608 | tf_op jit(solution)/shard_map/scatter | solution.py:146
  124.0 6.0 %fusion.69 = f32[1,4,2,32,128]{4,3,2,1,0:T(8,128)S(1)} fusion(bf16[4,2,2048,128]{3,2,1,0:T(8,128)(2,1)S(1)} %copy-done.1, pred[4,2048]{1,0:T(4,128)(4,1)S(1)} %get-tuple-element.48, f32[4,2,2048]{2,1,0:T(2,128)S(1)} %copy-done.24, bf16[4,2,2048,128]{3,2,1,0:T(8,128)(2,1)} %param.21, f32[4,2,32,2048]{3,2,1,0:T(8,128)S(1)} %copy-done.12, ...), kind=kOutput, calls=%fused_computation.63 | convolution fusion | flops 144179200 | bytes 10699776 | tf_op jit(solution)/shard_map/bhqk,bhkd->bhqd/dot_general | solution.py:26
  130.0 0.9 convolution_bitcast_fusion
  131.0 2.6 scatter_fusion.3
  133.6 7.2 %fusion.72 = f32[1,4,2,32,128]{4,3,2,1,0:T(8,128)S(1)} fusion(pred[4,2048]{1,0:T(4,128)(4,1)S(1)} %get-tuple-element.48, bf16[4,2,2048,128]{3,1,2,0:T(2,128)(2,1)} %scatter_fusion.3, f32[4,2,2048]{2,1,0:T(2,128)S(1)} %copy-done.24, bf16[4,2,2048,128]{3,2,1,0:T(8,128)(2,1)} %param.21, f32[4,2,32,2048]{3,2,1,0:T(8,128)} %get-tuple-element.58, ...), kind=kOutput, calls=%fused_computation.64 | convolution fusion | flops 144179200 | bytes 10699776 | tf_op jit(solution)/shard_map/bhqk,bhkd->bhqd/dot_general | solution.py:26
  140.8 1.9 convert_reduce_fusion.1
  143.0 1.0 fusion.63
  145.6 0.7 pad_maximum_fusion.2
  146.3 0.7 pad_maximum_fusion.4
  147.8 3.2 all-to-all-start.1
  151.7 5.7 %all-to-all-done.1 = f32[1,8,64]{2,0,1:T(1,128)S(1)} async-done(((f32[1,8,64]{2,0,1:T(1,128)}), f32[1,8,64]{2,0,1:T(1,128)S(1)}, u32[]{:S(2)}, u32[]{:S(2)}) %all-to-all-start.1) | async-done | bytes 2080 | tf_op jit(solution)/shard_map/all_to_all | solution.py:63
  157.4 3.3 all-to-all-start.4
  163.4 3.8 %all-to-all-done.4 = f32[1,8,64]{2,0,1:T(1,128)S(1)} async-done(((f32[1,8,64]{2,0,1:T(1,128)}), f32[1,8,64]{2,0,1:T(1,128)S(1)}, u32[]{:S(2)}, u32[]{:S(2)}) %all-to-all-start.4) | async-done | bytes 2080 | tf_op jit(solution)/shard_map/all_to_all | solution.py:63
  167.2 3.3 all-to-all-start.5
  170.5 6.4 %all-to-all-done.5 = f32[1,8,64]{2,0,1:T(1,128)S(1)} async-done(((f32[1,8,64]{2,0,1:T(1,128)}), f32[1,8,64]{2,0,1:T(1,128)S(1)}, u32[]{:S(2)}, u32[]{:S(2)}) %all-to-all-start.5) | async-done | bytes 2080 | tf_op jit(solution)/shard_map/all_to_all | solution.py:64
  176.9 3.3 all-to-all-start.8
  180.3 6.3 %all-to-all-done.8 = f32[1,8,64]{2,0,1:T(1,128)S(1)} async-done(((f32[1,8,64]{2,0,1:T(1,128)}), f32[1,8,64]{2,0,1:T(1,128)S(1)}, u32[]{:S(2)}, u32[]{:S(2)}) %all-to-all-start.8) | async-done | bytes 2080 | tf_op jit(solution)/shard_map/all_to_all | solution.py:64
  186.6 3.2 all-to-all-start.7
  189.9 6.3 %all-to-all-done.7 = f32[1,8,64]{2,0,1:T(1,128)S(1)} async-done(((f32[1,8,64]{2,0,1:T(1,128)}), f32[1,8,64]{2,0,1:T(1,128)S(1)}, u32[]{:S(2)}, u32[]{:S(2)}) %all-to-all-start.7) | async-done | bytes 2080 | tf_op jit(solution)/shard_map/all_to_all | solution.py:63
  196.2 3.4 %all-to-all-start = ((f32[1,512,128]{2,0,1:T(1,128)}), f32[1,512,128]{2,0,1:T(1,128)S(1)}, u32[]{:S(2)}, u32[]{:S(2)}) async-start(f32[1,512,128]{2,0,1:T(1,128)} %bitcast.6), calls=%async_computation | async-start | bytes 524288 | tf_op jit(solution)/shard_map/all_to_all | solution.py:65
  199.9 7.9 %all-to-all-done = f32[1,512,128]{2,0,1:T(1,128)S(1)} async-done(((f32[1,512,128]{2,0,1:T(1,128)}), f32[1,512,128]{2,0,1:T(1,128)S(1)}, u32[]{:S(2)}, u32[]{:S(2)}) %all-to-all-start) | async-done | bytes 262176 | tf_op jit(solution)/shard_map/all_to_all | solution.py:65
  207.8 3.4 %all-to-all-start.3 = ((f32[1,512,128]{2,0,1:T(1,128)}), f32[1,512,128]{2,0,1:T(1,128)S(1)}, u32[]{:S(2)}, u32[]{:S(2)}) async-start(f32[1,512,128]{2,0,1:T(1,128)} %bitcast.43), calls=%async_computation.3 | async-start | bytes 524288 | tf_op jit(solution)/shard_map/all_to_all | solution.py:65
  211.5 32.1 %all_gather.9 = bf16[512,128]{1,0:T(8,128)(2,1)S(1)} all-gather(bf16[64,128]{1,0:T(8,128)(2,1)S(1)} %divide_convert_fusion.2), channel_id=1, replica_groups=mesh['seq'=8,'tp'=4] {'seq'}, dimensions={0}, use_global_device_ids=true | all-gather | bytes 147456 | tf_op jit(solution)/shard_map/all_gather | solution.py:83
  243.7 3.0 fusion.171
  246.7 4.5 %all-to-all-start.6 = ((f32[1,512,128]{2,0,1:T(1,128)}), f32[1,512,128]{2,0,1:T(1,128)S(1)}, u32[]{:S(2)}, u32[]{:S(2)}) async-start(f32[1,512,128]{2,0,1:T(1,128)} %bitcast.80), calls=%async_computation.6 | async-start | bytes 524288 | tf_op jit(solution)/shard_map/all_to_all | solution.py:65
  251.5 32.0 %all_gather.10 = bf16[512,128]{1,0:T(8,128)(2,1)S(1)} all-gather(bf16[64,128]{1,0:T(8,128)(2,1)S(1)} %divide_convert_fusion.1), channel_id=1, replica_groups=mesh['seq'=8,'tp'=4] {'seq'}, dimensions={0}, use_global_device_ids=true | all-gather | bytes 147456 | tf_op jit(solution)/shard_map/all_gather | solution.py:83
  283.5 3.0 fusion.172
  286.8 30.5 %all_gather.11 = bf16[512,128]{1,0:T(8,128)(2,1)S(1)} all-gather(bf16[64,128]{1,0:T(8,128)(2,1)S(1)} %divide_convert_fusion), channel_id=1, replica_groups=mesh['seq'=8,'tp'=4] {'seq'}, dimensions={0}, use_global_device_ids=true | all-gather | bytes 147456 | tf_op jit(solution)/shard_map/all_gather | solution.py:83
  317.4 3.0 fusion.173
  320.4 14.8 %all-reduce.3 = (bf16[32,1024]{1,0:T(8,128)(2,1)S(1)}, bf16[32,1024]{1,0:T(8,128)(2,1)S(1)}, bf16[32,1024]{1,0:T(8,128)(2,1)S(1)}) all-reduce(f32[32,1024]{1,0:T(8,128)S(1)} %fusion.173, f32[32,1024]{1,0:T(8,128)S(1)} %fusion.172, f32[32,1024]{1,0:T(8,128)S(1)} %fusion.171), channel_id=1, replica_groups=mesh['seq'=8,'tp'=4] {'tp'}, use_global_device_ids=true, to_apply=%region_42.43 | all-reduce | flops 98304 | bytes 589824 | tf_op jit(solution)/shard_map/psum | solution.py:136
  (141 shorter events, 12.9 us)
Async XLA Ops:
  0.0 4.6 %copy-start.7 = (bf16[4,2,2048,128]{3,2,1,0:T(8,128)(2,1)S(1)}, bf16[4,2,2048,128]{3,2,1,0:T(8,128)(2,1)}, u32[]{:S(2)}) copy-start(bf16[4,2,2048,128]{3,2,1,0:T(8,128)(2,1)} %param.19) | copy-start | bytes 12582916
  4.6 2.0 copy-start.17
  4.6 2.0 copy-start.18
  4.6 2.1 copy-start.16
  6.7 4.0 %copy-start.2 = (bf16[4,2,2048,128]{3,2,1,0:T(8,128)(2,1)S(1)}, bf16[4,2,2048,128]{3,2,1,0:T(8,128)(2,1)}, u32[]{:S(2)}) copy-start(bf16[4,2,2048,128]{3,2,1,0:T(8,128)(2,1)} %copy.174) | copy-start | bytes 12582916
  6.7 4.0 %copy-start.22 = (f32[4,2,2048]{2,1,0:T(2,128)S(1)}, f32[4,2,2048]{2,1,0:T(2,128)}, u32[]{:S(2)}) copy-start(f32[4,2,2048]{2,1,0:T(2,128)} %param.22) | copy-start | bytes 196612
  16.6 1.3 copy-start.8
  16.6 9.3 %copy-start.14 = (bf16[1024,2,256]{2,1,0:T(2,128)(2,1)S(1)}, bf16[1024,2,256]{2,1,0:T(2,128)(2,1)}, u32[]{:S(2)}) copy-start(bf16[1024,2,256]{2,1,0:T(2,128)(2,1)} %param.14) | copy-start | bytes 3145732
  17.9 8.2 %copy-start.15 = (bf16[3,16,1024]{2,1,0:T(8,128)(2,1)S(1)}, bf16[3,16,1024]{2,1,0:T(8,128)(2,1)}, u32[]{:S(2)}) copy-start(bf16[3,16,1024]{2,1,0:T(8,128)(2,1)} %param.13) | copy-start | bytes 294916
  18.6 129.2 %all-to-all-start.2 = ((f32[1,8,64]{2,0,1:T(1,128)}), f32[1,8,64]{2,0,1:T(1,128)S(1)}, u32[]{:S(2)}, u32[]{:S(2)}) async-start(f32[1,8,64]{2,0,1:T(1,128)} %all_to_all.104), calls=%async_computation.2 | async-start | bytes 8192 | tf_op jit(solution)/shard_map/all_to_all | solution.py:64
  26.1 39.5 %copy-start.21 = (bf16[3,4,2,32,128]{4,3,2,1,0:T(8,128)(2,1)S(1)}, bf16[3,4,2,32,128]{4,3,2,1,0:T(8,128)(2,1)}, u32[]{:S(2)}) copy-start(bf16[3,4,2,32,128]{4,3,2,1,0:T(8,128)(2,1)} %param.16) | copy-start | bytes 589828
  69.3 13.3 %copy-start.23 = (f32[4,2,2048]{2,1,0:T(2,128)S(1)}, f32[4,2,2048]{2,1,0:T(2,128)}, u32[]{:S(2)}) copy-start(f32[4,2,2048]{2,1,0:T(2,128)} %param.22) | copy-start | bytes 196612
  82.6 8.5 %copy-start.6 = (bf16[4,2,2048,128]{3,1,2,0:T(2,128)(2,1)S(1)}, bf16[4,2,2048,128]{3,1,2,0:T(2,128)(2,1)}, u32[]{:S(2)}) copy-start(bf16[4,2,2048,128]{3,1,2,0:T(2,128)(2,1)} %scatter_fusion.2) | copy-start | bytes 12582916
  82.6 11.4 %copy-start.19 = (bf16[4,2,2048,128]{3,2,1,0:T(8,128)(2,1)S(1)}, bf16[4,2,2048,128]{3,2,1,0:T(8,128)(2,1)}, u32[]{:S(2)}) copy-start(bf16[4,2,2048,128]{3,2,1,0:T(8,128)(2,1)} %param.20) | copy-start | bytes 12582916
  91.1 2.9 copy-start.3
  100.2 2.8 copy-start
  103.1 1.6 copy-start.9
  103.1 2.8 copy-start.20
  103.1 2.8 copy-start.24
  113.4 10.6 %copy-start.1 = (bf16[4,2,2048,128]{3,2,1,0:T(8,128)(2,1)S(1)}, bf16[4,2,2048,128]{3,2,1,0:T(8,128)(2,1)}, u32[]{:S(2)}) copy-start(bf16[4,2,2048,128]{3,2,1,0:T(8,128)(2,1)} %scatter_fusion.1) | copy-start | bytes 12582916
  113.4 10.6 %copy-start.12 = (f32[4,2,32,2048]{3,2,1,0:T(8,128)S(1)}, f32[4,2,32,2048]{3,2,1,0:T(8,128)}, u32[]{:S(2)}) copy-start(f32[4,2,32,2048]{3,2,1,0:T(8,128)} %get-tuple-element.70) | copy-start | bytes 6291460
  124.0 6.0 %copy-start.4 = (f32[4,2,32,2048]{3,2,1,0:T(8,128)S(1)}, f32[4,2,32,2048]{3,2,1,0:T(8,128)}, u32[]{:S(2)}) copy-start(f32[4,2,32,2048]{3,2,1,0:T(8,128)} %get-tuple-element.68) | copy-start | bytes 6291460
  133.6 7.2 %copy-start.10 = (f32[4,2,32,2048]{3,2,1,0:T(8,128)S(1)}, f32[4,2,32,2048]{3,2,1,0:T(8,128)}, u32[]{:S(2)}) copy-start(f32[4,2,32,2048]{3,2,1,0:T(8,128)} %get-tuple-element.56) | copy-start | bytes 6291460
  133.6 7.2 %copy-start.11 = (f32[4,2,32,2048]{3,2,1,0:T(8,128)S(1)}, f32[4,2,32,2048]{3,2,1,0:T(8,128)}, u32[]{:S(2)}) copy-start(f32[4,2,32,2048]{3,2,1,0:T(8,128)} %get-tuple-element.58) | copy-start | bytes 6291460
  133.6 7.2 %copy-start.13 = (f32[4,2,32,2048]{3,2,1,0:T(8,128)S(1)}, f32[4,2,32,2048]{3,2,1,0:T(8,128)}, u32[]{:S(2)}) copy-start(f32[4,2,32,2048]{3,2,1,0:T(8,128)} %get-tuple-element.70) | copy-start | bytes 6291460
  140.8 2.2 copy-start.5
  147.8 9.7 %all-to-all-start.1 = ((f32[1,8,64]{2,0,1:T(1,128)}), f32[1,8,64]{2,0,1:T(1,128)S(1)}, u32[]{:S(2)}, u32[]{:S(2)}) async-start(f32[1,8,64]{2,0,1:T(1,128)} %all_to_all.101), calls=%async_computation.1 | async-start | bytes 8192 | tf_op jit(solution)/shard_map/all_to_all | solution.py:63
  157.4 9.8 %all-to-all-start.4 = ((f32[1,8,64]{2,0,1:T(1,128)}), f32[1,8,64]{2,0,1:T(1,128)S(1)}, u32[]{:S(2)}, u32[]{:S(2)}) async-start(f32[1,8,64]{2,0,1:T(1,128)} %all_to_all.109), calls=%async_computation.4 | async-start | bytes 8192 | tf_op jit(solution)/shard_map/all_to_all | solution.py:63
  167.2 9.7 %all-to-all-start.5 = ((f32[1,8,64]{2,0,1:T(1,128)}), f32[1,8,64]{2,0,1:T(1,128)S(1)}, u32[]{:S(2)}, u32[]{:S(2)}) async-start(f32[1,8,64]{2,0,1:T(1,128)} %all_to_all.112), calls=%async_computation.5 | async-start | bytes 8192 | tf_op jit(solution)/shard_map/all_to_all | solution.py:64
  176.9 9.7 %all-to-all-start.8 = ((f32[1,8,64]{2,0,1:T(1,128)}), f32[1,8,64]{2,0,1:T(1,128)S(1)}, u32[]{:S(2)}, u32[]{:S(2)}) async-start(f32[1,8,64]{2,0,1:T(1,128)} %all_to_all.120), calls=%async_computation.8 | async-start | bytes 8192 | tf_op jit(solution)/shard_map/all_to_all | solution.py:64
  186.6 9.7 %all-to-all-start.7 = ((f32[1,8,64]{2,0,1:T(1,128)}), f32[1,8,64]{2,0,1:T(1,128)S(1)}, u32[]{:S(2)}, u32[]{:S(2)}) async-start(f32[1,8,64]{2,0,1:T(1,128)} %all_to_all.117), calls=%async_computation.7 | async-start | bytes 8192 | tf_op jit(solution)/shard_map/all_to_all | solution.py:63
  196.2 11.6 %all-to-all-start = ((f32[1,512,128]{2,0,1:T(1,128)}), f32[1,512,128]{2,0,1:T(1,128)S(1)}, u32[]{:S(2)}, u32[]{:S(2)}) async-start(f32[1,512,128]{2,0,1:T(1,128)} %bitcast.6), calls=%async_computation | async-start | bytes 524288 | tf_op jit(solution)/shard_map/all_to_all | solution.py:65
  207.8 38.8 %all-to-all-start.3 = ((f32[1,512,128]{2,0,1:T(1,128)}), f32[1,512,128]{2,0,1:T(1,128)S(1)}, u32[]{:S(2)}, u32[]{:S(2)}) async-start(f32[1,512,128]{2,0,1:T(1,128)} %bitcast.43), calls=%async_computation.3 | async-start | bytes 524288 | tf_op jit(solution)/shard_map/all_to_all | solution.py:65
  246.7 39.8 %all-to-all-start.6 = ((f32[1,512,128]{2,0,1:T(1,128)}), f32[1,512,128]{2,0,1:T(1,128)S(1)}, u32[]{:S(2)}, u32[]{:S(2)}) async-start(f32[1,512,128]{2,0,1:T(1,128)} %bitcast.80), calls=%async_computation.6 | async-start | bytes 524288 | tf_op jit(solution)/shard_map/all_to_all | solution.py:65
where the time goes:
time: 337 us; the launch traced here: 336 us
  blocking collectives  148 us (44%)
  matrix products  62.7 us (19%)
  local copies, waits for them, and re-layouts  45.8 us (14%)
  waiting for transfers between devices  36.6 us (11%)
  starting transfers between devices  35 us (10%)
  other arithmetic  7.3 us (2%)
    all_gather x3, blocking collectives, spread_merge(): gathered = lax.all_gather(merged, 'seq', axis=0, tiled=True)  94.5 us
    psum x1, blocking collectives, per_device(): lax.psum(partial_kv, 'seq').astype(jnp.bfloat16)  38.5 us
    dot_general x12, matrix products, attend(): jnp.einsum('bhqd,bhkd->bhqk', queries, keys, preferred_element_type=jnp.f...  31.3 us
    dot_general x12, matrix products, attend(): jnp.einsum('bhqk,bhkd->bhqd', weights, values, preferred_element_type=jnp...  21.6 us
    all_to_all x3, waiting for transfers between devices, spread_merge(): lax.all_to_all(maxima, 'seq', split_axis=1, concat_axis=0, tiled=True)  15.9 us
    scatter x3, local copies, waits for them, and re-layouts, per_device(): values_cache.at[batch_rows, :, targets, :]  15.7 us
    scatter x3, local copies, waits for them, and re-layouts, per_device(): keys_cache.at[batch_rows, :, targets, :]  15.6 us
    psum x1, blocking collectives, per_device(): summed = lax.psum(projected, 'tp')  14.8 us
  transfers between devices with their start and end apart: 9, of which 6 were waited for; matrix products, arithmetic and copies ran while one was open for 26% of the time, Pallas kernels for 0%

commit v1 on v0

--- a/solution.py
+++ b/solution.py
@@ -116,7 +116,7 @@
     for turn_index in range(ROUNDS):
         partial_kv = jnp.dot(hidden_new[turn_index], flat_kv, preferred_element_type=jnp.float32)
         fresh_rows = (
-            lax.psum(partial_kv, "seq")
+            jnp.sum(lax.all_gather(partial_kv, "seq"), axis=0)
             .astype(jnp.bfloat16)
             .reshape(batch_size, R, head_count, 2, head_width)
         )

time: 337 us -> 424 us (1.26)
  blocking collectives: 148 us -> 201 us
  local copies, waits for them, and re-layouts: 45.8 us -> 73.7 us
    all_gather x0 -> x3, blocking collectives: none -> 92.8 us  [per_device(): lax.all_gather(partial_kv, 'seq')]
    psum x1 -> x0, blocking collectives: 38.5 us -> none  [per_device(): lax.psum(partial_kv, 'seq').astype(jnp.bfloat16)]
    scatter x3, local copies, waits for them, and re-layouts: 15.6 us -> 40.8 us  [per_device(): keys_cache.at[batch_rows, :, targets, :]]
    unnamed x53 -> x59, local copies, waits for them, and re-layouts: 9.41 us -> 11.4 us
  transfers between devices with their start and end apart: 9 -> 9, of which waited for: 6 -> 6; matrix products, arithmetic and copies ran while one was open for 26% -> 27% of each run, Pallas kernels for 0% -> 0%
where the time goes in v1:
time: 424 us; the launch traced here: 422 us
  blocking collectives  201 us (47%)
  local copies, waits for them, and re-layouts  73.7 us (17%)
  matrix products  64.6 us (15%)
  starting transfers between devices  37.9 us (9%)
  waiting for transfers between devices  36.6 us (9%)
  other arithmetic  7.38 us (2%)
    all_gather x3, blocking collectives, spread_merge(): gathered = lax.all_gather(merged, 'seq', axis=0, tiled=True)  93.6 us
    all_gather x3, blocking collectives, per_device(): lax.all_gather(partial_kv, 'seq')  92.8 us
    scatter x3, local copies, waits for them, and re-layouts, per_device(): keys_cache.at[batch_rows, :, targets, :]  40.8 us
    dot_general x12, matrix products, attend(): jnp.einsum('bhqd,bhkd->bhqk', queries, keys, preferred_element_type=jnp.f...  35.1 us
    dot_general x12, matrix products, attend(): jnp.einsum('bhqk,bhkd->bhqd', weights, values, preferred_element_type=jnp...  19.8 us
    all_to_all x3, waiting for transfers between devices, spread_merge(): lax.all_to_all(maxima, 'seq', split_axis=1, concat_axis=0, tiled=True)  16 us
    scatter x3, local copies, waits for them, and re-layouts, per_device(): values_cache.at[batch_rows, :, targets, :]  16 us
    psum x1, blocking collectives, per_device(): summed = lax.psum(projected, 'tp')  14.9 us
  transfers between devices with their start and end apart: 9, of which 6 were waited for; matrix products, arithmetic and copies ran while one was open for 27% of the time, Pallas kernels for 0%

profile of v1, /device:TPU:0, one launch (start us, length us, event | category | flops | bytes accessed | tf_op | source)
XLA Modules:
  0.0 422.1 jit_solution(213200153600396702)
XLA Ops:
  0.0 4.6 %copy.168 = bf16[4,2,2048,128]{3,2,1,0:T(8,128)(2,1)} copy(bf16[4,2,2048,128]{3,2,1,0:T(8,128)(2,1)} %param.18) | data formatting | bytes 8388608
  4.6 1.9 copy.169
  6.7 4.0 fusion.169
  10.7 5.9 %fusion.170 = (f32[4,2,32]{2,1,0:T(2,128)S(1)}, f32[4,2,32,2048]{3,2,1,0:T(8,128)S(1)}) fusion(bf16[3,4,2,32,128]{4,3,2,1,0:T(8,128)(2,1)} %param.16, bf16[4,2,2048,128]{3,2,1,0:T(8,128)(2,1)S(1)} %copy-done.2, pred[4,2048]{1,0:T(4,128)(4,1)S(1)} %get-tuple-element.45, f32[4,2,2048]{2,1,0:T(2,128)S(1)} %copy-done.24, bf16[4,2,2048,128]{3,2,1,0:T(8,128)(2,1)} %param.20), kind=kOutput, calls=%fused_computation.243 | convolution fusion | flops 144178944 | bytes 10634240 | tf_op jit(solution)/shard_map/bhqd,bhkd->bhqk/dot_general | solution.py:19
  16.6 0.9 convert_reduce_fusion.5
  18.7 7.3 %all-to-all-start.2 = ((f32[1,8,64]{2,0,1:T(1,128)}), f32[1,8,64]{2,0,1:T(1,128)S(1)}, u32[]{:S(2)}, u32[]{:S(2)}) async-start(f32[1,8,64]{2,0,1:T(1,128)} %all_to_all.104), calls=%async_computation.2 | async-start | bytes 8192 | tf_op jit(solution)/shard_map/all_to_all | solution.py:64
  27.5 31.3 %all-gather = f32[128,512]{1,0:T(8,128)S(1)} all-gather(f32[16,512]{1,0:T(8,128)S(1)} %fusion.115), channel_id=2, replica_groups=mesh['seq'=8,'tp'=4] {'seq'}, dimensions={0}, use_global_device_ids=true | all-gather | bytes 294912 | tf_op jit(solution)/shard_map/all_gather | solution.py:119
  59.2 30.7 %all-gather.1 = f32[128,512]{1,0:T(8,128)S(1)} all-gather(f32[16,512]{1,0:T(8,128)S(1)} %fusion.113), channel_id=3, replica_groups=mesh['seq'=8,'tp'=4] {'seq'}, dimensions={0}, use_global_device_ids=true | all-gather | bytes 294912 | tf_op jit(solution)/shard_map/all_gather | solution.py:119
  90.4 30.7 %all-gather.2 = f32[128,512]{1,0:T(8,128)S(1)} all-gather(f32[16,512]{1,0:T(8,128)S(1)} %fusion.111), channel_id=4, replica_groups=mesh['seq'=8,'tp'=4] {'seq'}, dimensions={0}, use_global_device_ids=true | all-gather | bytes 294912 | tf_op jit(solution)/shard_map/all_gather | solution.py:119
  123.2 2.7 scatter_fusion
  125.9 5.2 %fusion.167 = (f32[4,2,32]{2,1,0:T(2,128)S(1)}, f32[4,2,32,2048]{3,2,1,0:T(8,128)}) fusion(bf16[4,2,2048,128]{3,2,1,0:T(8,128)(2,1)} %scatter_fusion, bf16[3,4,2,32,128]{4,3,2,1,0:T(8,128)(2,1)S(1)} %copy-done.16, pred[4,2048]{1,0:T(4,128)(4,1)S(1)} %get-tuple-element.43), kind=kOutput, calls=%fused_computation.240 | convolution fusion | flops 135790336 | bytes 6366208 | tf_op jit(solution)/shard_map/bhqd,bhkd->bhqk/dot_general | solution.py:19
  131.1 6.8 %fusion.168 = (f32[4,2,32]{2,1,0:T(2,128)S(1)}, f32[4,2,32,2048]{3,2,1,0:T(8,128)}) fusion(bf16[3,4,2,32,128]{4,3,2,1,0:T(8,128)(2,1)S(1)} %copy-done.23, bf16[4,2,2048,128]{3,2,1,0:T(8,128)(2,1)S(1)} %copy-done.3, pred[4,2048]{1,0:T(4,128)(4,1)S(1)} %get-tuple-element.45, f32[4,2,2048]{2,1,0:T(2,128)S(1)} %copy-done.25, ...), kind=kOutput, calls=%fused_computation.241 | convolution fusion | flops 144178944 | bytes 10634240 | tf_op jit(solution)/shard_map/bhqd,bhkd->bhqk/dot_general | solution.py:19
  137.8 35.4 %copy.70 = bf16[4,2,2048,128]{3,1,2,0:T(2,128)(2,1)} copy(bf16[4,2,2048,128]{3,2,1,0:T(8,128)(2,1)S(1)} %copy-done.3) | data formatting | bytes 8388608 | tf_op jit(solution)/shard_map/scatter | solution.py:143
  173.4 2.7 scatter_fusion.2
  176.1 5.2 %fusion.161 = (f32[4,2,32]{2,1,0:T(2,128)S(1)}, f32[4,2,32,2048]{3,2,1,0:T(8,128)}) fusion(bf16[3,4,2,32,128]{4,3,2,1,0:T(8,128)(2,1)S(1)} %copy-done.16, bf16[4,2,2048,128]{3,1,2,0:T(2,128)(2,1)} %scatter_fusion.2, pred[4,2048]{1,0:T(4,128)(4,1)S(1)} %get-tuple-element.44), kind=kOutput, calls=%fused_computation.234 | convolution fusion | flops 135790336 | bytes 6366208 | tf_op jit(solution)/shard_map/bhqd,bhkd->bhqk/dot_general | solution.py:19
  181.3 7.0 %fusion.162 = (f32[4,2,32]{2,1,0:T(2,128)S(1)}, f32[4,2,32,2048]{3,2,1,0:T(8,128)}) fusion(bf16[3,4,2,32,128]{4,3,2,1,0:T(8,128)(2,1)S(1)} %copy-done.23, pred[4,2048]{1,0:T(4,128)(4,1)S(1)} %get-tuple-element.45, bf16[4,2,2048,128]{3,1,2,0:T(2,128)(2,1)S(1)} %copy-done.5, f32[4,2,2048]{2,1,0:T(2,128)S(1)} %copy-done.25, ...), kind=kOutput, calls=%fused_computation.235 | convolution fusion | flops 144178944 | bytes 10634240 | tf_op jit(solution)/shard_map/bhqd,bhkd->bhqk/dot_general | solution.py:19
  190.0 1.2 copy-done.20
  191.2 4.2 fusion.66
  195.4 2.7 scatter_fusion.1
  198.1 10.6 %copy.74 = bf16[4,2,2048,128]{3,1,2,0:T(2,128)(2,1)} copy(bf16[4,2,2048,128]{3,2,1,0:T(8,128)(2,1)} %scatter_fusion.1) | data formatting | bytes 8388608 | tf_op jit(solution)/shard_map/scatter | solution.py:146
  208.8 0.9 convolution_bitcast_fusion
  210.3 1.2 copy-done.21
  211.6 4.2 fusion.69
  215.8 2.7 scatter_fusion.3
  218.4 7.3 %fusion.72 = f32[1,4,2,32,128]{4,3,2,1,0:T(8,128)S(1)} fusion(pred[4,2048]{1,0:T(4,128)(4,1)S(1)} %get-tuple-element.45, bf16[4,2,2048,128]{3,1,2,0:T(2,128)(2,1)} %scatter_fusion.3, f32[4,2,2048]{2,1,0:T(2,128)} %param.23, bf16[4,2,2048,128]{3,2,1,0:T(8,128)(2,1)} %param.21, f32[4,2,32,2048]{3,2,1,0:T(8,128)} %get-tuple-element.55, ...), kind=kOutput, calls=%fused_computation.64 | convolution fusion | flops 144179200 | bytes 10699776 | tf_op jit(solution)/shard_map/bhqk,bhkd->bhqd/dot_general | solution.py:26
  225.7 1.9 convert_reduce_fusion.1
  227.9 1.0 fusion.63
  231.9 6.0 %all-to-all-start.1 = ((f32[1,8,64]{2,0,1:T(1,128)}), f32[1,8,64]{2,0,1:T(1,128)S(1)}, u32[]{:S(2)}, u32[]{:S(2)}) async-start(f32[1,8,64]{2,0,1:T(1,128)} %all_to_all.101), calls=%async_computation.1 | async-start | bytes 8192 | tf_op jit(solution)/shard_map/all_to_all | solution.py:63
  238.6 5.8 %all-to-all-done.1 = f32[1,8,64]{2,0,1:T(1,128)S(1)} async-done(((f32[1,8,64]{2,0,1:T(1,128)}), f32[1,8,64]{2,0,1:T(1,128)S(1)}, u32[]{:S(2)}, u32[]{:S(2)}) %all-to-all-start.1) | async-done | bytes 2080 | tf_op jit(solution)/shard_map/all_to_all | solution.py:63
  244.4 3.3 all-to-all-start.4
  248.4 5.7 %all-to-all-done.4 = f32[1,8,64]{2,0,1:T(1,128)S(1)} async-done(((f32[1,8,64]{2,0,1:T(1,128)}), f32[1,8,64]{2,0,1:T(1,128)S(1)}, u32[]{:S(2)}, u32[]{:S(2)}) %all-to-all-start.4) | async-done | bytes 2080 | tf_op jit(solution)/shard_map/all_to_all | solution.py:63
  254.1 3.3 all-to-all-start.7
  259.3 4.5 %all-to-all-done.7 = f32[1,8,64]{2,0,1:T(1,128)S(1)} async-done(((f32[1,8,64]{2,0,1:T(1,128)}), f32[1,8,64]{2,0,1:T(1,128)S(1)}, u32[]{:S(2)}, u32[]{:S(2)}) %all-to-all-start.7) | async-done | bytes 2080 | tf_op jit(solution)/shard_map/all_to_all | solution.py:63
  263.9 3.2 all-to-all-start.5
  267.2 6.4 %all-to-all-done.5 = f32[1,8,64]{2,0,1:T(1,128)S(1)} async-done(((f32[1,8,64]{2,0,1:T(1,128)}), f32[1,8,64]{2,0,1:T(1,128)S(1)}, u32[]{:S(2)}, u32[]{:S(2)}) %all-to-all-start.5) | async-done | bytes 2080 | tf_op jit(solution)/shard_map/all_to_all | solution.py:64
  273.5 3.3 all-to-all-start.8
  276.9 6.3 %all-to-all-done.8 = f32[1,8,64]{2,0,1:T(1,128)S(1)} async-done(((f32[1,8,64]{2,0,1:T(1,128)}), f32[1,8,64]{2,0,1:T(1,128)S(1)}, u32[]{:S(2)}, u32[]{:S(2)}) %all-to-all-start.8) | async-done | bytes 2080 | tf_op jit(solution)/shard_map/all_to_all | solution.py:64
  283.2 3.4 all-to-all-start.6
  286.8 7.9 %all-to-all-done.6 = f32[1,512,128]{2,0,1:T(1,128)S(1)} async-done(((f32[1,512,128]{2,0,1:T(1,128)}), f32[1,512,128]{2,0,1:T(1,128)S(1)}, u32[]{:S(2)}, u32[]{:S(2)}) %all-to-all-start.6) | async-done | bytes 262176 | tf_op jit(solution)/shard_map/all_to_all | solution.py:65
  294.8 3.4 all-to-all-start.3
  298.5 32.0 %all_gather.35 = bf16[512,128]{1,0:T(8,128)(2,1)S(1)} all-gather(bf16[64,128]{1,0:T(8,128)(2,1)S(1)} %divide_convert_fusion), channel_id=1, replica_groups=mesh['seq'=8,'tp'=4] {'seq'}, dimensions={0}, use_global_device_ids=true | all-gather | bytes 147456 | tf_op jit(solution)/shard_map/all_gather | solution.py:83
  330.6 4.6 %all-to-all-start = ((f32[1,512,128]{2,0,1:T(1,128)}), f32[1,512,128]{2,0,1:T(1,128)S(1)}, u32[]{:S(2)}, u32[]{:S(2)}) async-start(f32[1,512,128]{2,0,1:T(1,128)} %bitcast.6), calls=%async_computation | async-start | bytes 524288 | tf_op jit(solution)/shard_map/all_to_all | solution.py:65
  335.3 3.0 fusion.173
  338.4 31.1 %all_gather.32 = bf16[512,128]{1,0:T(8,128)(2,1)S(1)} all-gather(bf16[64,128]{1,0:T(8,128)(2,1)S(1)} %divide_convert_fusion.1), channel_id=1, replica_groups=mesh['seq'=8,'tp'=4] {'seq'}, dimensions={0}, use_global_device_ids=true | all-gather | bytes 147456 | tf_op jit(solution)/shard_map/all_gather | solution.py:83
  369.6 3.0 fusion.172
  372.9 30.5 %all_gather.29 = bf16[512,128]{1,0:T(8,128)(2,1)S(1)} all-gather(bf16[64,128]{1,0:T(8,128)(2,1)S(1)} %divide_convert_fusion.2), channel_id=1, replica_groups=mesh['seq'=8,'tp'=4] {'seq'}, dimensions={0}, use_global_device_ids=true | all-gather | bytes 147456 | tf_op jit(solution)/shard_map/all_gather | solution.py:83
  403.5 3.0 fusion.171
  406.5 14.9 %all-reduce.2 = (bf16[32,1024]{1,0:T(8,128)(2,1)S(1)}, bf16[32,1024]{1,0:T(8,128)(2,1)S(1)}, bf16[32,1024]{1,0:T(8,128)(2,1)S(1)}) all-reduce(f32[32,1024]{1,0:T(8,128)S(1)} %fusion.173, f32[32,1024]{1,0:T(8,128)S(1)} %fusion.172, f32[32,1024]{1,0:T(8,128)S(1)} %fusion.171), channel_id=1, replica_groups=mesh['seq'=8,'tp'=4] {'tp'}, use_global_device_ids=true, to_apply=%region_42.43 | all-reduce | flops 98304 | bytes 589824 | tf_op jit(solution)/shard_map/psum | solution.py:136
  (152 shorter events, 16.5 us)
Async XLA Ops:
  0.0 4.6 %copy-start.7 = (bf16[4,2,2048,128]{3,2,1,0:T(8,128)(2,1)S(1)}, bf16[4,2,2048,128]{3,2,1,0:T(8,128)(2,1)}, u32[]{:S(2)}) copy-start(bf16[4,2,2048,128]{3,2,1,0:T(8,128)(2,1)} %param.19) | copy-start | bytes 12582916
  4.6 1.9 copy-start.17
  4.6 1.9 copy-start.18
  4.6 2.1 copy-start.16
  6.7 4.0 copy-start.2
  6.7 4.0 copy-start.24
  16.6 1.4 copy-start.8
  16.6 9.8 %copy-start.14 = (bf16[1024,2,256]{2,1,0:T(2,128)(2,1)S(1)}, bf16[1024,2,256]{2,1,0:T(2,128)(2,1)}, u32[]{:S(2)}) copy-start(bf16[1024,2,256]{2,1,0:T(2,128)(2,1)} %param.14) | copy-start | bytes 3145732
  18.0 8.7 %copy-start.15 = (bf16[3,16,1024]{2,1,0:T(8,128)(2,1)S(1)}, bf16[3,16,1024]{2,1,0:T(8,128)(2,1)}, u32[]{:S(2)}) copy-start(bf16[3,16,1024]{2,1,0:T(8,128)(2,1)} %param.13) | copy-start | bytes 294916
  18.7 213.2 %all-to-all-start.2 = ((f32[1,8,64]{2,0,1:T(1,128)}), f32[1,8,64]{2,0,1:T(1,128)S(1)}, u32[]{:S(2)}, u32[]{:S(2)}) async-start(f32[1,8,64]{2,0,1:T(1,128)} %all_to_all.104), calls=%async_computation.2 | async-start | bytes 8192 | tf_op jit(solution)/shard_map/all_to_all | solution.py:64
  26.7 32.3 %copy-start.22 = (bf16[3,4,2,32,128]{4,3,2,1,0:T(8,128)(2,1)S(1)}, bf16[3,4,2,32,128]{4,3,2,1,0:T(8,128)(2,1)}, u32[]{:S(2)}) copy-start(bf16[3,4,2,32,128]{4,3,2,1,0:T(8,128)(2,1)} %param.16) | copy-start | bytes 589828
  27.4 95.6 %copy-start.19 = (s32[4]{0:T(128)S(1)}, s32[4]{0:T(128)}, u32[]{:S(2)}) copy-start(s32[4]{0:T(128)} %get-tuple-element.47) | copy-start | bytes 52
  125.9 5.2 %copy-start.3 = (bf16[4,2,2048,128]{3,2,1,0:T(8,128)(2,1)S(1)}, bf16[4,2,2048,128]{3,2,1,0:T(8,128)(2,1)}, u32[]{:S(2)}) copy-start(bf16[4,2,2048,128]{3,2,1,0:T(8,128)(2,1)} %scatter_fusion) | copy-start | bytes 12582916
  125.9 5.2 %copy-start.23 = (bf16[3,4,2,32,128]{4,3,2,1,0:T(8,128)(2,1)S(1)}, bf16[3,4,2,32,128]{4,3,2,1,0:T(8,128)(2,1)}, u32[]{:S(2)}) copy-start(bf16[3,4,2,32,128]{4,3,2,1,0:T(8,128)(2,1)} %param.16) | copy-start | bytes 589828
  125.9 5.2 %copy-start.25 = (f32[4,2,2048]{2,1,0:T(2,128)S(1)}, f32[4,2,2048]{2,1,0:T(2,128)}, u32[]{:S(2)}) copy-start(f32[4,2,2048]{2,1,0:T(2,128)} %param.22) | copy-start | bytes 196612
  176.1 5.2 %copy-start.5 = (bf16[4,2,2048,128]{3,1,2,0:T(2,128)(2,1)S(1)}, bf16[4,2,2048,128]{3,1,2,0:T(2,128)(2,1)}, u32[]{:S(2)}) copy-start(bf16[4,2,2048,128]{3,1,2,0:T(2,128)(2,1)} %scatter_fusion.2) | copy-start | bytes 12582916
  181.3 7.0 %copy-start = (bf16[4,2,2048,128]{3,2,1,0:T(8,128)(2,1)S(1)}, bf16[4,2,2048,128]{3,2,1,0:T(8,128)(2,1)}, u32[]{:S(2)}) copy-start(bf16[4,2,2048,128]{3,2,1,0:T(8,128)(2,1)} %copy.169) | copy-start | bytes 12582916
  188.4 1.6 copy-start.9
  188.4 2.8 copy-start.20
  188.4 2.8 copy-start.26
  198.1 10.6 %copy-start.1 = (bf16[4,2,2048,128]{3,2,1,0:T(8,128)(2,1)S(1)}, bf16[4,2,2048,128]{3,2,1,0:T(8,128)(2,1)}, u32[]{:S(2)}) copy-start(bf16[4,2,2048,128]{3,2,1,0:T(8,128)(2,1)} %scatter_fusion.1) | copy-start | bytes 12582916
  198.1 10.6 %copy-start.4 = (f32[4,2,32,2048]{3,2,1,0:T(8,128)S(1)}, f32[4,2,32,2048]{3,2,1,0:T(8,128)}, u32[]{:S(2)}) copy-start(f32[4,2,32,2048]{3,2,1,0:T(8,128)} %get-tuple-element.65) | copy-start | bytes 6291460
  208.7 1.6 copy-start.10
  208.7 2.8 copy-start.21
  208.7 2.8 copy-start.27
  218.4 7.3 %copy-start.11 = (f32[4,2,32,2048]{3,2,1,0:T(8,128)S(1)}, f32[4,2,32,2048]{3,2,1,0:T(8,128)}, u32[]{:S(2)}) copy-start(f32[4,2,32,2048]{3,2,1,0:T(8,128)} %get-tuple-element.67) | copy-start | bytes 6291460
  218.4 7.3 %copy-start.12 = (f32[4,2,32,2048]{3,2,1,0:T(8,128)S(1)}, f32[4,2,32,2048]{3,2,1,0:T(8,128)}, u32[]{:S(2)}) copy-start(f32[4,2,32,2048]{3,2,1,0:T(8,128)} %get-tuple-element.53) | copy-start | bytes 6291460
  218.4 7.3 %copy-start.13 = (f32[4,2,32,2048]{3,2,1,0:T(8,128)S(1)}, f32[4,2,32,2048]{3,2,1,0:T(8,128)}, u32[]{:S(2)}) copy-start(f32[4,2,32,2048]{3,2,1,0:T(8,128)} %get-tuple-element.55) | copy-start | bytes 6291460
  225.7 2.2 copy-start.6
  231.9 12.5 %all-to-all-start.1 = ((f32[1,8,64]{2,0,1:T(1,128)}), f32[1,8,64]{2,0,1:T(1,128)S(1)}, u32[]{:S(2)}, u32[]{:S(2)}) async-start(f32[1,8,64]{2,0,1:T(1,128)} %all_to_all.101), calls=%async_computation.1 | async-start | bytes 8192 | tf_op jit(solution)/shard_map/all_to_all | solution.py:63
  244.4 9.7 %all-to-all-start.4 = ((f32[1,8,64]{2,0,1:T(1,128)}), f32[1,8,64]{2,0,1:T(1,128)S(1)}, u32[]{:S(2)}, u32[]{:S(2)}) async-start(f32[1,8,64]{2,0,1:T(1,128)} %all_to_all.109), calls=%async_computation.4 | async-start | bytes 8192 | tf_op jit(solution)/shard_map/all_to_all | solution.py:63
  254.1 9.8 %all-to-all-start.7 = ((f32[1,8,64]{2,0,1:T(1,128)}), f32[1,8,64]{2,0,1:T(1,128)S(1)}, u32[]{:S(2)}, u32[]{:S(2)}) async-start(f32[1,8,64]{2,0,1:T(1,128)} %all_to_all.117), calls=%async_computation.7 | async-start | bytes 8192 | tf_op jit(solution)/shard_map/all_to_all | solution.py:63
  263.9 9.7 %all-to-all-start.5 = ((f32[1,8,64]{2,0,1:T(1,128)}), f32[1,8,64]{2,0,1:T(1,128)S(1)}, u32[]{:S(2)}, u32[]{:S(2)}) async-start(f32[1,8,64]{2,0,1:T(1,128)} %all_to_all.112), calls=%async_computation.5 | async-start | bytes 8192 | tf_op jit(solution)/shard_map/all_to_all | solution.py:64
  273.5 9.7 %all-to-all-start.8 = ((f32[1,8,64]{2,0,1:T(1,128)}), f32[1,8,64]{2,0,1:T(1,128)S(1)}, u32[]{:S(2)}, u32[]{:S(2)}) async-start(f32[1,8,64]{2,0,1:T(1,128)} %all_to_all.120), calls=%async_computation.8 | async-start | bytes 8192 | tf_op jit(solution)/shard_map/all_to_all | solution.py:64
  283.2 11.6 %all-to-all-start.6 = ((f32[1,512,128]{2,0,1:T(1,128)}), f32[1,512,128]{2,0,1:T(1,128)S(1)}, u32[]{:S(2)}, u32[]{:S(2)}) async-start(f32[1,512,128]{2,0,1:T(1,128)} %bitcast.82), calls=%async_computation.6 | async-start | bytes 524288 | tf_op jit(solution)/shard_map/all_to_all | solution.py:65
  294.8 35.8 %all-to-all-start.3 = ((f32[1,512,128]{2,0,1:T(1,128)}), f32[1,512,128]{2,0,1:T(1,128)S(1)}, u32[]{:S(2)}, u32[]{:S(2)}) async-start(f32[1,512,128]{2,0,1:T(1,128)} %bitcast.44), calls=%async_computation.3 | async-start | bytes 524288 | tf_op jit(solution)/shard_map/all_to_all | solution.py:65
  330.6 42.0 %all-to-all-start = ((f32[1,512,128]{2,0,1:T(1,128)}), f32[1,512,128]{2,0,1:T(1,128)S(1)}, u32[]{:S(2)}, u32[]{:S(2)}) async-start(f32[1,512,128]{2,0,1:T(1,128)} %bitcast.6), calls=%async_computation | async-start | bytes 524288 | tf_op jit(solution)/shard_map/all_to_all | solution.py:65
